TPU v7x, 32 devices: a whole 2x2x4 slice. The times are simulated.
32 devices in a mesh: ep: 8 (over z, x), tp: 4 (over y, core).
Axes of the slice: x: 2, y: 2, z: 4, core: 2. Of those that a mesh axis runs over, the one named last changes fastest.
Arguments:
- tokens: bfloat16 [16384, 768], P(('ep', 'tp')), may hold values from -6 to 6
- d_out: bfloat16 [16384, 768], P(('ep', 'tp')), may hold values from -6 to 6
- segment: int32 [16384], P(('ep', 'tp')), may hold values from -1 to 15, as said below
- route: int32 [16384, 1], P(('ep', 'tp')), may hold values from 0 to 15; in each aligned block of 512 rows (0 to 511, 512 to 1023, ...) at most 48 rows name the same one
- gain_one: bfloat16 [768], replicated, may hold values from 0.5 to 1.5
- w_in: bfloat16 [768, 3072], replicated, may hold values from -0.21875 to 0.21875
- conv_w: bfloat16 [4, 1536], replicated, may hold values from -3 to 3
- conv_b: bfloat16 [1536], replicated, may hold values from -3 to 3
- w_x: bfloat16 [1536, 80], replicated, may hold values from -0.15625 to 0.15625
- w_dt: bfloat16 [48, 1536], replicated, may hold values from -0.875 to 0.875
- b_dt: bfloat16 [1536], replicated, may hold values from -6 to -2
- a_log: bfloat16 [16, 1536], replicated, may hold values from 0 to 2.765625
- d_skip: bfloat16 [1536], replicated, may hold values from 0.5 to 1.5
- w_out: bfloat16 [1536, 768], replicated, may hold values from -0.15625 to 0.15625
- gain_two: bfloat16 [768], replicated, may hold values from 0.5 to 1.5
- w_router: bfloat16 [768, 16], replicated, may hold values from -0.15625 to 0.15625
- w_up: bfloat16 [16, 768, 3072], P('ep', None, 'tp'), may hold values from -0.21875 to 0.21875
- w_down: bfloat16 [16, 3072, 768], P('ep', 'tp'), may hold values from -1.75 to 1.75
Outputs:
- block_out: bfloat16 [16384, 768], P(('ep', 'tp'))
- d_tokens: float32 [16384, 768], P(('ep', 'tp'))
- counts: int32 [2, 16], replicated
- g_gain_one: float32 [768], replicated
- g_w_in: float32 [768, 3072], replicated
- g_conv_w: float32 [4, 1536], replicated
- g_conv_b: float32 [1536], replicated
- g_w_x: float32 [1536, 80], replicated
- g_w_dt: float32 [48, 1536], replicated
- g_b_dt: float32 [1536], replicated
- g_a_log: float32 [16, 1536], replicated
- g_d_skip: float32 [1536], replicated
- g_w_out: float32 [1536, 768], replicated
- g_gain_two: float32 [768], replicated
- g_w_router: float32 [768, 16], replicated
- g_w_up: float32 [16, 768, 3072], P('ep', None, 'tp')
- g_w_down: float32 [16, 3072, 768], P('ep', 'tp')
Inputs may be any that keep to these rules, and one draw needn't show every extreme that they name: `segment`: in each device's block of 512 tokens the samples are numbered 0, 1, 2 in order up to at most 15, each a run of consecutive positions beginning with the block's first position; padding tokens (-1) follow the last sample. No sample crosses a block. In every draw some block holds one sample of all 512 tokens, and some block reaches the largest number. `route`: within the tokens of one device, no expert is named by more than 48 tokens, padding included; some device reaches 48 for some expert.
All inputs are finite; a program needn't handle non-finite values.
Results may differ from a plain program's by a relative error of at most 0.0092.
Values may be sent and summed in bfloat16 or wider, within the bound.
A program may use at most 576 MiB of HBM per device.

v0:
```python
from functools import partial
import jax
import jax.numpy as jnp
from jax import lax
from jax.sharding import PartitionSpec as P

SCAN_BLOCK = 16
EPS = 1e-06
HIGH = lax.Precision.HIGHEST


def prefix(part, axis, combine, identity):
    place = lax.axis_index(axis)
    gathered = lax.all_gather(part, axis)
    state = jnp.zeros_like(part) + jnp.asarray(identity, part.dtype)

    def one(lap, state):
        return combine(state, lax.dynamic_index_in_dim(gathered, lap, 0, False))

    return lax.fori_loop(0, place, one, state)


def rms_scale(values, gain):
    return values * lax.rsqrt(jnp.mean(values * values, axis=-1, keepdims=True) + EPS) * gain


def sample_masks(segment, taps):
    length = segment.shape[0]
    masks = []
    for shift in range(taps):
        earlier = jnp.concatenate([jnp.full((shift,), -2, jnp.int32), segment[: length - shift]])
        masks.append((earlier == segment).astype(jnp.float32)[:, None])
    return masks


def causal_conv(inner, conv_w, conv_b, masks):
    taps = conv_w.shape[0]
    length = inner.shape[0]
    total = conv_b[None, :] + conv_w[taps - 1][None, :] * inner
    for shift in range(1, taps):
        moved = jnp.concatenate(
            [jnp.zeros((shift, inner.shape[1]), jnp.float32), inner[: length - shift]], axis=0
        )
        total = total + conv_w[taps - 1 - shift][None, :] * moved * masks[shift]
    return total


def combine_pairs(first, second):
    return (first[0] * second[0], second[0] * first[1] + second[1])


def to_blocks(values, blocks):
    length = values.shape[0]
    return jnp.swapaxes(values.reshape((blocks, length // blocks) + values.shape[1:]), 0, 1)


def selective_scan(step, in_b, out_c, conv, keep, rates):
    length, width = conv.shape
    blocks = length // SCAN_BLOCK
    states = rates.shape[0]
    step_p = to_blocks(step, blocks)
    inb_p = to_blocks(in_b, blocks)
    outc_p = to_blocks(out_c, blocks)
    conv_p = to_blocks(conv, blocks)
    keep_p = to_blocks(keep, blocks)

    def terms_at(step_t, inb_t, conv_t, keep_t):
        decay = keep_t[:, None, None] * jnp.exp(step_t[:, None, :] * rates[None])
        source = inb_t[:, :, None] * (step_t * conv_t)[:, None, :]
        return (decay, source)

    def first_pass(carry, item):
        decay, source = terms_at(item[0], item[1], item[2], item[3])
        return ((decay * carry[0] + source, decay * carry[1]), None)

    zero_state = jnp.zeros((blocks, states, width), jnp.float32)
    (block_ends, products), _ = lax.scan(
        jax.checkpoint(first_pass),
        (zero_state, jnp.ones_like(zero_state)),
        (step_p, inb_p, conv_p, keep_p),
    )
    _, reached = lax.associative_scan(combine_pairs, (products, block_ends), axis=0)
    starts = jnp.concatenate([jnp.zeros_like(reached[:1]), reached[:-1]], axis=0)

    def second_pass(state, item):
        decay, source = terms_at(item[0], item[1], item[2], item[3])
        state = decay * state + source
        return (state, jnp.sum(item[4][:, :, None] * state, axis=1))

    _, outputs = lax.scan(
        jax.checkpoint(second_pass), starts, (step_p, inb_p, conv_p, keep_p, outc_p)
    )
    return jnp.swapaxes(outputs, 0, 1).reshape(length, width)


def middle(inner, gate_z, conv_w, conv_b, w_x, w_dt, b_dt, a_log, d_skip, masks):
    conv = jax.nn.silu(causal_conv(inner, conv_w, conv_b, masks))
    proj = jnp.dot(conv, w_x, precision=HIGH)
    rank_dt = w_dt.shape[0]
    states = a_log.shape[0]
    step = jax.nn.softplus(jnp.dot(proj[:, :rank_dt], w_dt, precision=HIGH) + b_dt)
    in_b = proj[:, rank_dt : rank_dt + states]
    out_c = proj[:, rank_dt + states :]
    rates = -jnp.exp(a_log)
    ssm_out = selective_scan(step, in_b, out_c, conv, masks[1][:, 0], rates)
    result = ssm_out + d_skip * conv
    return result * jax.nn.silu(gate_z)


def add_counts(earlier, later):
    return earlier + later


def contract_rows(left, right):
    return lax.dot_general(
        left, right, (((0,), (0,)), ((), ())), preferred_element_type=jnp.float32
    )


def local(
    tokens,
    d_out,
    segment,
    route,
    gain_one,
    w_in,
    conv_w,
    conv_b,
    w_x,
    w_dt,
    b_dt,
    a_log,
    d_skip,
    w_out,
    gain_two,
    w_router,
    w_up,
    w_down,
):
    length, width = tokens.shape
    inner_w = w_in.shape[1] // 2
    experts = w_router.shape[1]
    local_experts = w_up.shape[0]
    groups = lax.axis_size("ep")
    slots = 3 * length // (2 * experts)
    capacity = 5 * length * lax.axis_size("ep") * lax.axis_size("tp") // (4 * experts)
    token_f = tokens.astype(jnp.float32)
    valid = (segment >= 0).astype(jnp.float32)[:, None]
    masks = sample_masks(segment, conv_w.shape[0])
    small_f = [
        item.astype(jnp.float32) for item in (conv_w, conv_b, w_x, w_dt, b_dt, a_log, d_skip)
    ]
    normed_one, norm_one_pull = jax.vjp(rms_scale, token_f, gain_one.astype(jnp.float32))
    normed_low = normed_one.astype(jnp.bfloat16)
    both = jnp.dot(normed_low, w_in, preferred_element_type=jnp.float32)

    def middle_fixed(inner, gate_z, conv_wf, conv_bf, w_xf, w_dtf, b_dtf, a_logf, d_skipf):
        return middle(inner, gate_z, conv_wf, conv_bf, w_xf, w_dtf, b_dtf, a_logf, d_skipf, masks)

    gated, middle_pull = jax.vjp(
        middle_fixed,
        both[:, :inner_w],
        both[:, inner_w:],
        small_f[0],
        small_f[1],
        small_f[2],
        small_f[3],
        small_f[4],
        small_f[5],
        small_f[6],
    )
    gated_low = gated.astype(jnp.bfloat16)
    mixed = jnp.dot(gated_low, w_out, preferred_element_type=jnp.float32)
    after_mix = token_f + mixed * valid
    normed_two, norm_two_pull = jax.vjp(rms_scale, after_mix, gain_two.astype(jnp.float32))
    pick_int = (
        (route == jnp.arange(experts, dtype=jnp.int32)[None, :]) & (segment >= 0)[:, None]
    ).astype(jnp.int32)
    picks = pick_int.astype(jnp.float32)

    def router(normed_in, router_w):
        probs = jax.nn.softmax(jnp.dot(normed_in, router_w, precision=HIGH), axis=-1)
        return jnp.sum(probs * picks, axis=-1)

    gate, router_pull = jax.vjp(router, normed_two, w_router.astype(jnp.float32))
    local_count = jnp.sum(pick_int, axis=0)
    prior = prefix(local_count, ("ep", "tp"), add_counts, jnp.zeros_like(local_count))
    local_rank = jnp.sum(jnp.cumsum(pick_int, axis=0) * pick_int, axis=1) - 1
    global_rank = jnp.sum(pick_int * prior[None, :], axis=1) + local_rank
    kept = (segment >= 0) & (global_rank < capacity)
    slot_id = jnp.where(kept, route[:, 0] * slots + local_rank, -1)
    dispatch = (jnp.arange(experts * slots, dtype=jnp.int32)[:, None] == slot_id[None, :]).astype(
        jnp.bfloat16
    )
    expert_in = normed_two.astype(jnp.bfloat16)
    outgoing = jnp.dot(dispatch, expert_in, preferred_element_type=jnp.float32).astype(jnp.bfloat16)
    outgoing = outgoing.reshape(groups, local_experts, slots, width)
    received = lax.all_to_all(outgoing, "ep", split_axis=0, concat_axis=2, tiled=True)
    full_up, full_down = (w_up, w_down)
    expert_rows = lax.all_gather(received, "tp", axis=2, tiled=True)
    hidden_pre = jnp.einsum(
        "axrd,xdf->axrf", expert_rows, full_up, preferred_element_type=jnp.float32
    )
    gelu_value, gelu_pull = jax.vjp(partial(jax.nn.gelu, approximate=False), hidden_pre)
    hidden_low = gelu_value.astype(jnp.bfloat16)
    terms = jnp.einsum("axrf,xfd->axrd", hidden_low, full_down, preferred_element_type=jnp.float32)
    expert_out = lax.psum_scatter(terms, "tp", scatter_dimension=2, tiled=True)
    returned = lax.all_to_all(
        expert_out.astype(jnp.bfloat16), "ep", split_axis=2, concat_axis=0, tiled=True
    )
    returned = returned.reshape(experts * slots, width)
    token_out = contract_rows(dispatch, returned)
    keep_f = kept.astype(jnp.float32)[:, None]
    weighting = gate[:, None] * keep_f
    final = after_mix + weighting * token_out
    upstream = d_out.astype(jnp.float32)
    d_token_out = (weighting * upstream).astype(jnp.bfloat16)
    d_slots = jnp.dot(dispatch, d_token_out, preferred_element_type=jnp.float32).astype(
        jnp.bfloat16
    )
    d_slots = d_slots.reshape(groups, local_experts, slots, width)
    d_gate = keep_f[:, 0] * jnp.sum(upstream * token_out, axis=1)
    d_received = lax.all_to_all(d_slots, "ep", split_axis=0, concat_axis=2, tiled=True)
    d_rows_all = lax.all_gather(d_received, "tp", axis=2, tiled=True)
    again = jnp.einsum("axrd,xdf->axrf", expert_rows, full_up, preferred_element_type=jnp.float32)
    again_value, gelu_back = jax.vjp(partial(jax.nn.gelu, approximate=False), again)
    hidden_back = again_value.astype(jnp.bfloat16)
    grad_down = jnp.einsum(
        "axrf,axrd->xfd", hidden_back, d_rows_all, preferred_element_type=jnp.float32
    )
    d_hidden = jnp.einsum(
        "axrd,xfd->axrf", d_rows_all, full_down, preferred_element_type=jnp.float32
    )
    d_pre = gelu_back(d_hidden)[0].astype(jnp.bfloat16)
    grad_up = jnp.einsum("axrd,axrf->xdf", expert_rows, d_pre, preferred_element_type=jnp.float32)
    row_terms = jnp.einsum("axrf,xdf->axrd", d_pre, full_up, preferred_element_type=jnp.float32)
    d_expert_in = lax.psum_scatter(row_terms, "tp", scatter_dimension=2, tiled=True)
    d_back = lax.all_to_all(
        d_expert_in.astype(jnp.bfloat16), "ep", split_axis=2, concat_axis=0, tiled=True
    )
    d_normed = contract_rows(dispatch, d_back.reshape(experts * slots, width))
    d_norm_router, grad_router = router_pull(d_gate)
    d_after, grad_gain_two = norm_two_pull(d_normed + d_norm_router)
    d_after = d_after + upstream
    d_mixed = (d_after * valid).astype(jnp.bfloat16)
    grad_out = contract_rows(gated_low, d_mixed)
    d_gated = lax.dot_general(
        d_mixed, w_out, (((1,), (1,)), ((), ())), preferred_element_type=jnp.float32
    )
    middle_grads = middle_pull(d_gated)
    d_both = jnp.concatenate([middle_grads[0], middle_grads[1]], axis=1).astype(jnp.bfloat16)
    grad_in = contract_rows(normed_low, d_both)
    d_normed_one = lax.dot_general(
        d_both, w_in, (((1,), (1,)), ((), ())), preferred_element_type=jnp.float32
    )
    d_tokens_norm, grad_gain_one = norm_one_pull(d_normed_one)
    d_tokens = d_after + d_tokens_norm
    held = jnp.sum(pick_int * kept.astype(jnp.int32)[:, None], axis=0)
    count_f = jnp.stack([local_count, local_count - held]).astype(jnp.float32)
    summed = lax.psum(
        (
            grad_gain_one,
            grad_in,
            middle_grads[2],
            middle_grads[3],
            middle_grads[4],
            middle_grads[5],
            middle_grads[6],
            middle_grads[7],
            middle_grads[8],
            grad_out,
            grad_gain_two,
            grad_router,
            count_f,
        ),
        ("ep", "tp"),
    )
    return (
        final.astype(jnp.bfloat16),
        d_tokens,
        summed[12].astype(jnp.int32),
        summed[0],
        summed[1],
        summed[2],
        summed[3],
        summed[4],
        summed[5],
        summed[6],
        summed[7],
        summed[8],
        summed[9],
        summed[10],
        summed[11],
        grad_up,
        grad_down,
    )


def solution(mesh):
    in_specs = (
        P(("ep", "tp"), None),
        P(("ep", "tp"), None),
        P(("ep", "tp")),
        P(("ep", "tp"), None),
        P(),
        P(),
        P(),
        P(),
        P(),
        P(),
        P(),
        P(),
        P(),
        P(),
        P(),
        P(),
        P("ep", None, "tp"),
        P("ep", "tp", None),
    )
    out_specs = (
        P(("ep", "tp"), None),
        P(("ep", "tp"), None),
        P(),
        P(),
        P(),
        P(),
        P(),
        P(),
        P(),
        P(),
        P(),
        P(),
        P(),
        P(),
        P(),
        P("ep", None, "tp"),
        P("ep", "tp", None),
    )
    return jax.shard_map(local, mesh=mesh, in_specs=in_specs, out_specs=out_specs, check_vma=False)
```

profile of v0, /device:TPU:0, one launch (start us, length us, event | category | flops | bytes accessed | tf_op | source)
XLA Modules:
  0.0 2524.6 jit_solution(8566170891215152491)
XLA Ops:
  47.1 16.5 broadcast.378.clone
  63.6 16.4 broadcast.378.clone.1
  80.0 250.0 %while.93 = (s32[]{:T(128)}, f32[32,16,1536]{2,1,0:T(8,128)}, f32[32,16,1536]{2,1,0:T(8,128)}, f32[16,32,16,1536]{3,2,1,0:T(8,128)}, f32[16,32,16,1536]{3,2,1,0:...) while((s32[]{:T(128)}, f32[32,16,1536]{2,1,0:T(8,128)}, ...), condition=%wide.region_2.3_spmd.clone, body=%wide.region_1.2_spmd.clone.sunk | while | flops 7913475 | bytes 26647568 | solution.py:77
  379.9 10.9 pad.393
  393.5 10.9 pad.299
  409.9 16.5 broadcast.378
  428.5 197.7 %while.91 = (s32[]{:T(128)}, f32[32,16,1536]{2,1,0:T(8,128)}, f32[16,32,1536]{2,1,0:T(8,128)}, f32[16,32,16,1536]{3,2,1,0:T(8,128)}, f32[16,32]{1,0:T(8,128)S(1)...) while((s32[]{:T(128)}, f32[32,16,1536]{2,1,0:T(8,128)}, ...), condition=%wide.region_5.6_spmd, body=%wide.region_3.5_spmd.sunk | while | flops 5505026 | bytes 14661117 | solution.py:90
  637.7 42.1 %all-reduce.62 = s32[512]{0:T(512)S(1)} all-reduce(s32[512]{0:T(512)S(1)} %dynamic-update-slice), channel_id=2, replica_groups=mesh['ep'=8,'tp'=4] {'ep','tp'}, use_global_device_ids=true, to_apply=%add.62 | all-reduce | flops 512 | bytes 4096
  684.5 33.4 %all_to_all.66 = bf16[8,2,48,768]{3,2,1,0:T(8,128)(2,1)S(1)} all-to-all(bf16[8,2,48,768]{3,2,1,0:T(8,128)(2,1)S(1)} %bitcast.381), channel_id=1, replica_groups=mesh['ep'=8,'tp'=4] {'ep'}, dimensions={0} | all-to-all | bytes 2359296 | tf_op jit(solution)/shard_map/all_to_all | solution.py:198
  719.1 36.3 %all-gather.4.cloned.1.call-done = bf16[1,2,1536,768]{3,2,1,0:T(8,128)(2,1)} async-done(((bf16[1,2,384,768]{3,2,1,0:T(8,128)(2,1)}), bf16[1,2,1536,768]{3,2,1,0:T(8,128)(2,1)}) %all-gather.4.cloned.1.call-update) | async-done | bytes 4718608 | tf_op jit(solution)/shard_map/all_gather | solution.py:200
  765.5 25.9 %convolution_bitcast_fusion.1 = f32[1,2,1536,768]{3,2,1,0:T(8,128)} fusion(bf16[2,768,768]{2,1,0:T(8,128)(2,1)S(1)} %copy-done, f32[2,1536,768]{2,1,0:T(8,128)S(1)} %fusion.38), kind=kOutput, calls=%fused_computation.96 | convolution fusion | flops 3777232896 | bytes 21233664 | tf_op jit(solution)/shard_map/axrf,xfd->axrd/dot_general | solution.py:206
  791.5 78.6 %reduce-scatter.3.cloned.1.call-done = f32[1,2,384,768]{3,2,1,0:T(8,128)} async-done(((f32[1,2,1536,768]{3,2,1,0:T(8,128)}), f32[1,2,384,768]{3,2,1,0:T(8,128)}) %reduce-scatter.3.cloned.1.call-update) | async-done | bytes 2359312 | tf_op jit(solution)/shard_map/reduce_scatter | solution.py:207
  883.8 24.4 all-to-all-done.1
  913.2 32.5 %all_to_all.67 = bf16[8,2,48,768]{3,2,1,0:T(8,128)(2,1)S(1)} all-to-all(bf16[8,2,48,768]{3,2,1,0:T(8,128)(2,1)S(1)} %bitcast.382), channel_id=1, replica_groups=mesh['ep'=8,'tp'=4] {'ep'}, dimensions={0} | all-to-all | bytes 2359296 | tf_op jit(solution)/shard_map/all_to_all | solution.py:223
  946.9 35.3 %all-gather.6.cloned.1.call-done = bf16[1,2,1536,768]{3,2,1,0:T(8,128)(2,1)} async-done(((bf16[1,2,384,768]{3,2,1,0:T(8,128)(2,1)}), bf16[1,2,1536,768]{3,2,1,0:T(8,128)(2,1)}) %all-gather.6.cloned.1.call-update) | async-done | bytes 4718608 | tf_op jit(solution)/shard_map/all_gather | solution.py:224
  982.2 26.4 %fusion.18 = bf16[1,2,1536,768]{3,2,1,0:T(8,128)(2,1)S(1)} fusion(f32[2,1536,768]{2,1,0:T(8,128)} %copy-done.159, bf16[2,768,768]{2,1,0:T(8,128)(2,1)S(1)} %copy-done, bf16[1,2,1536,768]{3,2,1,0:T(8,128)(2,1)} %all-gather.6.cloned.1.call-done), kind=kOutput, calls=%fused_computation.74 | convolution fusion | flops 3793747968 | bytes 21233664 | tf_op jit(solution)/shard_map/axrd,xfd->axrf/dot_general | solution.py:231
  1017.2 78.6 %reduce-scatter.5.cloned.1.call-done = f32[1,2,384,768]{3,2,1,0:T(8,128)} async-done(((f32[1,2,1536,768]{3,2,1,0:T(8,128)}), f32[1,2,384,768]{3,2,1,0:T(8,128)}) %reduce-scatter.5.cloned.1.call-update) | async-done | bytes 2359312 | tf_op jit(solution)/shard_map/reduce_scatter | solution.py:237
  1108.0 26.1 %all-to-all-done.3 = bf16[1,2,384,768]{3,1,0,2:T(2,128)(2,1)S(1)} async-done(((bf16[1,2,384,768]{3,1,0,2:T(2,128)(2,1)}), bf16[1,2,384,768]{3,1,0,2:T(2,128)(2,1)S(1)}, u32[]{:S(2)}, u32[]{:S(2)}) %all-to-all-start.3) | async-done | bytes 1179680 | tf_op jit(solution)/shard_map/all_to_all | solution.py:238
  1158.5 280.6 %while.94 = (s32[]{:T(128)}, f32[16,1536]{1,0:T(8,128)}, f32[32,16,1536]{2,1,0:T(8,128)}, f32[16,32,1536]{2,1,0:T(8,128)}, f32[16,32,16]{2,1,0:T(8,128)}, /*inde...) while((s32[]{:T(128)}, f32[16,1536]{1,0:T(8,128)}, ...), condition=%wide.region_28.29_spmd.clone, body=%wide.region_22.28_spmd.clone.sunk | while | flops 17423364 | bytes 28472580 | solution.py:90
  1533.6 10.9 pad.270
  1589.6 183.8 %while.95 = (s32[]{:T(128)}, f32[16,1536]{1,0:T(8,128)S(1)}, f32[32,16,1536]{2,1,0:T(8,128)}, f32[32,16,1536]{2,1,0:T(8,128)S(1)}, f32[16,32,1536]{2,1,0:T(8,128...) while((s32[]{:T(128)}, f32[16,1536]{1,0:T(8,128)S(1)}, ...), condition=%wide.region_34.35_spmd.clone, body=%wide.region_29.34_spmd.clone.sunk | while | flops 13491716 | bytes 67070592 | solution.py:77
  1839.8 25.3 %fusion.34 = f32[2,768,768]{2,1,0:T(8,128)} fusion(bf16[1,2,1536,768]{3,2,1,0:T(8,128)(2,1)S(1)} %bitcast.403, f32[2,1536,768]{2,1,0:T(8,128)} %copy-done.159), kind=kOutput, calls=%fused_computation.103 | convolution fusion | flops 3777232896 | bytes 18874368 | tf_op jit(solution)/shard_map/axrf,axrd->xfd/dot_general | solution.py:228
  1866.6 81.4 %all-reduce.68.cloned.1.call-done = (f32[2,16]{1,0:T(2,128)}, f32[768]{0:T(1024)}, f32[4,1536]{1,0:T(4,128)}, f32[1536]{0:T(1024)}, f32[1536]{0:T(1024)}, /*inde...) async-done(((f32[2,16]{1,0:T(2,128)}, f32[768]{0:T(1024)}, f32[4,1536]{1,0:T(4,128)}, f32[1536]{0:T(1024)}, f32[1536]{0:T(1024)}, /*index=5*/f32[1536]{0:T(1024)}, ...) | async-done | bytes 98448 | tf_op jit(solution)/shard_map/psum | solution.py:260
  1949.3 550.1 %all-reduce.70.cloned.1.call-done = (f32[768,3072]{1,0:T(8,128)}, f32[1536,80]{0,1:T(8,128)}, f32[48,1536]{1,0:T(8,128)}, f32[16,1536]{1,0:T(8,128)}, f32[1536,768]{1,0:T(8,128)}) async-done(((f32[768,3072]{1,0:T(8,128)}, f32[1536,80]{0,1:T(8,128)}, f32[48,1536]{1,0:T(8,128)}, f32[16,1536]{1,0:T(8,128)}, f32[1536,768]{1,0:T(8,128)}), (f32[768,3072]{1,0:T(8,128)}, f32[1536,80]{0,1:T(8,128)}, ...) | async-done | bytes 15040528 | tf_op jit(solution)/shard_map/psum | solution.py:260
  (1377 shorter events, 1327.0 us)
Async XLA Ops:
  7.2 758.3 %copy-start = (bf16[2,768,768]{2,1,0:T(8,128)(2,1)S(1)}, bf16[2,768,768]{2,1,0:T(8,128)(2,1)}, u32[]{:S(2)}) copy-start(bf16[2,768,768]{2,1,0:T(8,128)(2,1)} %param.45) | copy-start | bytes 7077892
  7.2 748.2 %all-gather.4.cloned.1.call-start = ((), (), s32[]{:S(2)}) async-start(), calls=%async_computation.6 | async-start | bytes 5898240 | tf_op jit(solution)/shard_map/all_gather | solution.py:200
  22.2 659.3 %copy-start.120 = (pred[512]{0:T(512)(128)(4,1)}, pred[512]{0:T(512)(128)(4,1)S(1)}, u32[]{:S(2)}) copy-start(pred[512]{0:T(512)(128)(4,1)S(1)} %get-tuple-element.1214) | copy-start | bytes 1540
  634.5 47.6 %copy-start.150 = (bf16[768]{0:T(1024)(128)(2,1)S(1)}, bf16[768]{0:T(1024)(128)(2,1)}, u32[]{:S(2)}) copy-start(bf16[768]{0:T(1024)(128)(2,1)} %param.42) | copy-start | bytes 4612
  682.1 36.9 %copy-start.135 = (pred[512]{0:T(512)(128)(4,1)}, pred[512]{0:T(512)(128)(4,1)S(1)}, u32[]{:S(2)}) copy-start(pred[512]{0:T(512)(128)(4,1)S(1)} %get-tuple-element.1204) | copy-start | bytes 1540
  682.1 36.9 %copy-start.151 = (s32[512]{0:T(512)}, s32[512]{0:T(512)S(1)}, u32[]{:S(2)}) copy-start(s32[512]{0:T(512)S(1)} %add_select_fusion) | copy-start | bytes 6148
  719.0 151.0 %reduce-scatter.3.cloned.1.call-start = ((), (), s32[]{:S(2)}) async-start(), calls=%async_computation.7 | async-start | bytes 11796480 | tf_op jit(solution)/shard_map/reduce_scatter | solution.py:207
  874.1 34.1 %all-to-all-start.1 = ((bf16[1,2,384,768]{3,1,0,2:T(2,128)(2,1)}), bf16[1,2,384,768]{3,1,0,2:T(2,128)(2,1)S(1)}, u32[]{:S(2)}, u32[]{:S(2)}) async-start(bf16[1,2,384,768]{3,1,0,2:T(2,128)(2,1)} %copy.110), calls=%async_computation.2 | async-start | bytes 2359296 | tf_op jit(solution)/shard_map/all_to_all | solution.py:208
  879.6 102.6 %all-gather.6.cloned.1.call-start = ((), (), s32[]{:S(2)}) async-start(), calls=%async_computation.8 | async-start | bytes 5898240 | tf_op jit(solution)/shard_map/all_gather | solution.py:224
  946.8 149.0 %reduce-scatter.5.cloned.1.call-start = ((), (), s32[]{:S(2)}) async-start(), calls=%async_computation.9 | async-start | bytes 11796480 | tf_op jit(solution)/shard_map/reduce_scatter | solution.py:237
  982.2 28.6 %copy-start.156 = (bf16[2,768,768]{2,1,0:T(8,128)(2,1)S(1)}, bf16[2,768,768]{2,1,0:T(8,128)(2,1)}, u32[]{:S(2)}) copy-start(bf16[2,768,768]{2,1,0:T(8,128)(2,1)} %param.44) | copy-start | bytes 7077892
  1100.0 34.1 %all-to-all-start.3 = ((bf16[1,2,384,768]{3,1,0,2:T(2,128)(2,1)}), bf16[1,2,384,768]{3,1,0,2:T(2,128)(2,1)S(1)}, u32[]{:S(2)}, u32[]{:S(2)}) async-start(bf16[1,2,384,768]{3,1,0,2:T(2,128)(2,1)} %copy.114), calls=%async_computation.5 | async-start | bytes 2359296 | tf_op jit(solution)/shard_map/all_to_all | solution.py:238
  1105.5 842.5 %all-reduce.68.cloned.1.call-start = ((), (), s32[]{:S(2)}) async-start(), calls=%async_computation.10 | async-start | bytes 215040 | tf_op jit(solution)/shard_map/psum | solution.py:260
  1468.0 15.4 copy-start.79
  1468.0 17.5 copy-start.26
  1468.0 17.5 slice-start.8
  1490.7 13.7 copy-start.63
  1826.0 673.3 %all-reduce.70.cloned.1.call-start = ((), (), s32[]{:S(2)}) async-start(), calls=%async_computation.11 | async-start | bytes 30081024 | tf_op jit(solution)/shard_map/psum | solution.py:260
  1839.8 25.3 %copy-start.127 = (f32[512]{0:T(512)S(1)}, f32[512]{0:T(512)}, u32[]{:S(2)}) copy-start(f32[512]{0:T(512)} %copy-done.126) | copy-start | bytes 6148
  1839.8 25.3 %copy-start.28 = (f32[512,768]{1,0:T(8,128)S(1)}, f32[512,768]{1,0:T(8,128)}, u32[]{:S(2)}) copy-start(f32[512,768]{1,0:T(8,128)} %copy-done.27) | copy-start | bytes 4718596
  1839.8 25.3 %copy-start.48 = (bf16[512,768]{1,0:T(8,128)(2,1)S(1)}, bf16[512,768]{1,0:T(8,128)(2,1)}, u32[]{:S(2)}) copy-start(bf16[512,768]{1,0:T(8,128)(2,1)} %param.28) | copy-start | bytes 2359300
  1839.8 25.3 %copy-start.76 = (f32[512,768]{1,0:T(8,128)S(1)}, f32[512,768]{1,0:T(8,128)}, u32[]{:S(2)}) copy-start(f32[512,768]{1,0:T(8,128)} %get-tuple-element.1305) | copy-start | bytes 4718596
  2499.4 14.7 slice-start.5
  2500.8 13.3 slice-start.6
  (278 other events, 1053.5 us)
Sparse Core Ops, SparseCore 0:
  719.2 36.1 all-gather.3
  791.6 78.4 reduce-scatter.2
  946.9 35.2 all-gather.5
  1017.4 78.4 reduce-scatter.4
  1826.2 121.8 all-reduce.67
  1956.6 542.7 all-reduce.69
where the time goes:
time: 2540 us; the launch traced here: 2520 us
  waiting for transfers between devices  911 us (36%)
  local copies, waits for them, and re-layouts  676 us (27%)
  other arithmetic  638 us (25%)
  matrix products  161 us (6%)
  blocking collectives  108 us (4%)
    psum x2, waiting for transfers between devices, local(): lax.psum((grad_gain_one, grad_in, middle_grads[2], middle_grads[3], middl...  631 us
    mul x32, other arithmetic, first_pass(): return ((decay * carry[0] + source, decay * carry[1]), None)  151 us
    pad x32, local copies, waits for them, and re-layouts, selective_scan(): lax.associative_scan(combine_pairs, (products, block_ends), axis=0)  124 us
    squeeze x112, local copies, waits for them, and re-layouts, selective_scan(): lax.scan(jax.checkpoint(first_pass), (zero_state, jnp.ones_like(zero_stat...  124 us
    dynamic_update_slice x16, other arithmetic, selective_scan(): lax.scan(jax.checkpoint(first_pass), (zero_state, jnp.ones_like(zero_stat...  103 us
    reduce_sum x32, other arithmetic, terms_at(): decay = keep_t[:, None, None] * jnp.exp(step_t[:, None, :] * rates[None])  98.2 us
    squeeze x32, local copies, waits for them, and re-layouts, selective_scan(): lax.scan(jax.checkpoint(second_pass), starts, (step_p, inb_p, conv_p, kee...  89.3 us
    reduce_sum x16, other arithmetic, second_pass(): return (state, jnp.sum(item[4][:, :, None] * state, axis=1))  80.5 us
  transfers between devices with their start and end apart: 8, of which 8 were waited for; matrix products, arithmetic and copies ran while one was open for 2% of the time, Pallas kernels for 0%

commit v1 on v0

--- a/solution.py
+++ b/solution.py
@@ -258,22 +258,25 @@
     held = jnp.sum(pick_int * kept.astype(jnp.int32)[:, None], axis=0)
     count_f = jnp.stack([local_count, local_count - held]).astype(jnp.float32)
     summed = lax.psum(
-        (
-            grad_gain_one,
-            grad_in,
-            middle_grads[2],
-            middle_grads[3],
-            middle_grads[4],
-            middle_grads[5],
-            middle_grads[6],
-            middle_grads[7],
-            middle_grads[8],
-            grad_out,
-            grad_gain_two,
-            grad_router,
-            count_f,
+        lax.psum(
+            (
+                grad_gain_one,
+                grad_in,
+                middle_grads[2],
+                middle_grads[3],
+                middle_grads[4],
+                middle_grads[5],
+                middle_grads[6],
+                middle_grads[7],
+                middle_grads[8],
+                grad_out,
+                grad_gain_two,
+                grad_router,
+                count_f,
+            ),
+            "tp",
         ),
-        ("ep", "tp"),
+        "ep",
     )
     return (
         final.astype(jnp.bfloat16),

time: 2540 us -> 2710 us (1.067)
  waiting for transfers between devices: 911 us -> 1080 us
    psum x0 -> x2, waiting for transfers between devices: none -> 509 us  [local(): lax.psum(lax.psum((grad_gain_one, grad_in, middle_grads[2], middle_grads[...]
    psum x2, waiting for transfers between devices: 631 us -> 294 us  [local(): lax.psum((grad_gain_one, grad_in, middle_grads[2], middle_grads[3], middl...]
  transfers between devices with their start and end apart: 8 -> 10, of which waited for: 8 -> 10; matrix products, arithmetic and copies ran while one was open for 2% -> 2% of each run, Pallas kernels for 0% -> 0%
where the time goes in v1:
time: 2710 us; the launch traced here: 2700 us
  waiting for transfers between devices  1080 us (40%)
  local copies, waits for them, and re-layouts  677 us (25%)
  other arithmetic  638 us (24%)
  matrix products  161 us (6%)
  blocking collectives  108 us (4%)
    psum x2, waiting for transfers between devices, local(): lax.psum(lax.psum((grad_gain_one, grad_in, middle_grads[2], middle_grads[...  509 us
    psum x2, waiting for transfers between devices, local(): lax.psum((grad_gain_one, grad_in, middle_grads[2], middle_grads[3], middl...  294 us
    mul x32, other arithmetic, first_pass(): return ((decay * carry[0] + source, decay * carry[1]), None)  152 us
    squeeze x112, local copies, waits for them, and re-layouts, selective_scan(): lax.scan(jax.checkpoint(first_pass), (zero_state, jnp.ones_like(zero_stat...  124 us
    pad x32, local copies, waits for them, and re-layouts, selective_scan(): lax.associative_scan(combine_pairs, (products, block_ends), axis=0)  124 us
    dynamic_update_slice x16, other arithmetic, selective_scan(): lax.scan(jax.checkpoint(first_pass), (zero_state, jnp.ones_like(zero_stat...  103 us
    reduce_sum x32, other arithmetic, terms_at(): decay = keep_t[:, None, None] * jnp.exp(step_t[:, None, :] * rates[None])  98.3 us
    squeeze x32, local copies, waits for them, and re-layouts, selective_scan(): lax.scan(jax.checkpoint(second_pass), starts, (step_p, inb_p, conv_p, kee...  89.3 us
  transfers between devices with their start and end apart: 10, of which 10 were waited for; matrix products, arithmetic and copies ran while one was open for 2% of the time, Pallas kernels for 0%

profile of v1, /device:TPU:0, one launch (start us, length us, event | category | flops | bytes accessed | tf_op | source)
XLA Modules:
  0.0 2697.0 jit_solution(458874853621745407)
XLA Ops:
  47.2 16.4 broadcast.378.clone
  63.6 16.4 broadcast.378.clone.1
  80.0 250.3 %while.93 = (s32[]{:T(128)}, f32[32,16,1536]{2,1,0:T(8,128)}, f32[32,16,1536]{2,1,0:T(8,128)}, f32[16,32,16,1536]{3,2,1,0:T(8,128)}, f32[16,32,16,1536]{3,2,1,0:...) while((s32[]{:T(128)}, f32[32,16,1536]{2,1,0:T(8,128)}, ...), condition=%wide.region_2.3_spmd.clone, body=%wide.region_1.2_spmd.clone.sunk | while | flops 7913475 | bytes 26647568 | solution.py:77
  380.3 10.9 pad.393
  410.3 16.5 broadcast.378
  428.9 197.7 %while.91 = (s32[]{:T(128)}, f32[32,16,1536]{2,1,0:T(8,128)}, f32[16,32,1536]{2,1,0:T(8,128)}, f32[16,32,16,1536]{3,2,1,0:T(8,128)}, f32[16,32]{1,0:T(8,128)S(1)...) while((s32[]{:T(128)}, f32[32,16,1536]{2,1,0:T(8,128)}, ...), condition=%wide.region_5.6_spmd, body=%wide.region_3.5_spmd.sunk | while | flops 5505026 | bytes 14661117 | solution.py:90
  638.2 42.1 %all-reduce.62 = s32[512]{0:T(512)S(1)} all-reduce(s32[512]{0:T(512)S(1)} %dynamic-update-slice), channel_id=2, replica_groups=mesh['ep'=8,'tp'=4] {'ep','tp'}, use_global_device_ids=true, to_apply=%add.62 | all-reduce | flops 512 | bytes 4096
  684.9 33.5 %all_to_all.66 = bf16[8,2,48,768]{3,2,1,0:T(8,128)(2,1)S(1)} all-to-all(bf16[8,2,48,768]{3,2,1,0:T(8,128)(2,1)S(1)} %bitcast.381), channel_id=1, replica_groups=mesh['ep'=8,'tp'=4] {'ep'}, dimensions={0} | all-to-all | bytes 2359296 | tf_op jit(solution)/shard_map/all_to_all | solution.py:198
  719.6 36.3 %all-gather.4.cloned.1.call-done = bf16[1,2,1536,768]{3,2,1,0:T(8,128)(2,1)} async-done(((bf16[1,2,384,768]{3,2,1,0:T(8,128)(2,1)}), bf16[1,2,1536,768]{3,2,1,0:T(8,128)(2,1)}) %all-gather.4.cloned.1.call-update) | async-done | bytes 4718608 | tf_op jit(solution)/shard_map/all_gather | solution.py:200
  766.0 25.9 convolution_bitcast_fusion.1
  792.0 78.6 %reduce-scatter.3.cloned.1.call-done = f32[1,2,384,768]{3,2,1,0:T(8,128)} async-done(((f32[1,2,1536,768]{3,2,1,0:T(8,128)}), f32[1,2,384,768]{3,2,1,0:T(8,128)}) %reduce-scatter.3.cloned.1.call-update) | async-done | bytes 2359312 | tf_op jit(solution)/shard_map/reduce_scatter | solution.py:207
  884.3 24.3 all-to-all-done.1
  913.6 32.5 %all_to_all.67 = bf16[8,2,48,768]{3,2,1,0:T(8,128)(2,1)S(1)} all-to-all(bf16[8,2,48,768]{3,2,1,0:T(8,128)(2,1)S(1)} %bitcast.382), channel_id=1, replica_groups=mesh['ep'=8,'tp'=4] {'ep'}, dimensions={0} | all-to-all | bytes 2359296 | tf_op jit(solution)/shard_map/all_to_all | solution.py:223
  947.3 35.3 %all-gather.6.cloned.1.call-done = bf16[1,2,1536,768]{3,2,1,0:T(8,128)(2,1)} async-done(((bf16[1,2,384,768]{3,2,1,0:T(8,128)(2,1)}), bf16[1,2,1536,768]{3,2,1,0:T(8,128)(2,1)}) %all-gather.6.cloned.1.call-update) | async-done | bytes 4718608 | tf_op jit(solution)/shard_map/all_gather | solution.py:224
  982.6 26.5 fusion.18
  1017.7 78.6 %reduce-scatter.5.cloned.1.call-done = f32[1,2,384,768]{3,2,1,0:T(8,128)} async-done(((f32[1,2,1536,768]{3,2,1,0:T(8,128)}), f32[1,2,384,768]{3,2,1,0:T(8,128)}) %reduce-scatter.5.cloned.1.call-update) | async-done | bytes 2359312 | tf_op jit(solution)/shard_map/reduce_scatter | solution.py:237
  1108.5 26.1 all-to-all-done.3
  1159.0 281.2 %while.94 = (s32[]{:T(128)}, f32[16,1536]{1,0:T(8,128)}, f32[32,16,1536]{2,1,0:T(8,128)}, f32[16,32,1536]{2,1,0:T(8,128)}, f32[16,32,16]{2,1,0:T(8,128)}, /*inde...) while((s32[]{:T(128)}, f32[16,1536]{1,0:T(8,128)}, ...), condition=%wide.region_28.29_spmd.clone, body=%wide.region_22.28_spmd.clone.sunk | while | flops 17423364 | bytes 28472580 | solution.py:90
  1590.8 183.8 %while.95 = (s32[]{:T(128)}, f32[16,1536]{1,0:T(8,128)S(1)}, f32[32,16,1536]{2,1,0:T(8,128)}, f32[32,16,1536]{2,1,0:T(8,128)S(1)}, f32[16,32,1536]{2,1,0:T(8,128...) while((s32[]{:T(128)}, f32[16,1536]{1,0:T(8,128)S(1)}, ...), condition=%wide.region_34.35_spmd.clone, body=%wide.region_29.34_spmd.clone.sunk | while | flops 13491716 | bytes 67070592 | solution.py:77
  1830.8 24.9 all-reduce.76.cloned.1.call-done
  1855.8 268.7 %all-reduce.78.cloned.1.call-done = (f32[768,3072]{1,0:T(8,128)}, f32[1536,80]{0,1:T(8,128)}, f32[48,1536]{1,0:T(8,128)}, f32[16,1536]{1,0:T(8,128)}, f32[1536,768]{1,0:T(8,128)}) async-done(((f32[768,3072]{1,0:T(8,128)}, f32[1536,80]{0,1:T(8,128)}, f32[48,1536]{1,0:T(8,128)}, f32[16,1536]{1,0:T(8,128)}, f32[1536,768]{1,0:T(8,128)}), (f32[768,3072]{1,0:T(8,128)}, f32[1536,80]{0,1:T(8,128)}, ...) | async-done | bytes 15040528 | tf_op jit(solution)/shard_map/psum | solution.py:261
  2134.6 25.2 fusion.34
  2161.5 38.3 %all-reduce.72.cloned.1.call-done = (f32[2,16]{1,0:T(2,128)}, f32[768]{0:T(1024)}, f32[4,1536]{1,0:T(4,128)}, f32[1536]{0:T(1024)}, f32[1536]{0:T(1024)}, /*inde...) async-done(((f32[2,16]{1,0:T(2,128)}, f32[768]{0:T(1024)}, f32[4,1536]{1,0:T(4,128)}, f32[1536]{0:T(1024)}, f32[1536]{0:T(1024)}, /*index=5*/f32[1536]{0:T(1024)}, ...) | async-done | bytes 98448 | tf_op jit(solution)/shard_map/psum | solution.py:260
  2201.0 470.7 %all-reduce.74.cloned.1.call-done = (f32[768,3072]{1,0:T(8,128)}, f32[1536,80]{0,1:T(8,128)}, f32[48,1536]{1,0:T(8,128)}, f32[16,1536]{1,0:T(8,128)}, f32[1536,768]{1,0:T(8,128)}) async-done(((f32[768,3072]{1,0:T(8,128)}, f32[1536,80]{0,1:T(8,128)}, f32[48,1536]{1,0:T(8,128)}, f32[16,1536]{1,0:T(8,128)}, f32[1536,768]{1,0:T(8,128)}), (f32[768,3072]{1,0:T(8,128)}, f32[1536,80]{0,1:T(8,128)}, ...) | async-done | bytes 15040528 | tf_op jit(solution)/shard_map/psum | solution.py:260
  (1383 shorter events, 1350.1 us)
Async XLA Ops:
  7.2 758.8 %copy-start = (bf16[2,768,768]{2,1,0:T(8,128)(2,1)S(1)}, bf16[2,768,768]{2,1,0:T(8,128)(2,1)}, u32[]{:S(2)}) copy-start(bf16[2,768,768]{2,1,0:T(8,128)(2,1)} %param.45) | copy-start | bytes 7077892
  7.2 748.6 %all-gather.4.cloned.1.call-start = ((), (), s32[]{:S(2)}) async-start(), calls=%async_computation.6 | async-start | bytes 5898240 | tf_op jit(solution)/shard_map/all_gather | solution.py:200
  22.3 659.6 %copy-start.120 = (pred[512]{0:T(512)(128)(4,1)}, pred[512]{0:T(512)(128)(4,1)S(1)}, u32[]{:S(2)}) copy-start(pred[512]{0:T(512)(128)(4,1)S(1)} %get-tuple-element.1227) | copy-start | bytes 1540
  634.9 47.6 %copy-start.150 = (bf16[768]{0:T(1024)(128)(2,1)S(1)}, bf16[768]{0:T(1024)(128)(2,1)}, u32[]{:S(2)}) copy-start(bf16[768]{0:T(1024)(128)(2,1)} %param.42) | copy-start | bytes 4612
  682.5 37.0 %copy-start.135 = (pred[512]{0:T(512)(128)(4,1)}, pred[512]{0:T(512)(128)(4,1)S(1)}, u32[]{:S(2)}) copy-start(pred[512]{0:T(512)(128)(4,1)S(1)} %get-tuple-element.1217) | copy-start | bytes 1540
  682.5 37.0 %copy-start.151 = (s32[512]{0:T(512)}, s32[512]{0:T(512)S(1)}, u32[]{:S(2)}) copy-start(s32[512]{0:T(512)S(1)} %add_select_fusion) | copy-start | bytes 6148
  719.5 151.0 %reduce-scatter.3.cloned.1.call-start = ((), (), s32[]{:S(2)}) async-start(), calls=%async_computation.7 | async-start | bytes 11796480 | tf_op jit(solution)/shard_map/reduce_scatter | solution.py:207
  874.5 34.1 %all-to-all-start.1 = ((bf16[1,2,384,768]{3,1,0,2:T(2,128)(2,1)}), bf16[1,2,384,768]{3,1,0,2:T(2,128)(2,1)S(1)}, u32[]{:S(2)}, u32[]{:S(2)}) async-start(bf16[1,2,384,768]{3,1,0,2:T(2,128)(2,1)} %copy.110), calls=%async_computation.2 | async-start | bytes 2359296 | tf_op jit(solution)/shard_map/all_to_all | solution.py:208
  880.1 102.6 %all-gather.6.cloned.1.call-start = ((), (), s32[]{:S(2)}) async-start(), calls=%async_computation.8 | async-start | bytes 5898240 | tf_op jit(solution)/shard_map/all_gather | solution.py:224
  947.2 149.0 %reduce-scatter.5.cloned.1.call-start = ((), (), s32[]{:S(2)}) async-start(), calls=%async_computation.9 | async-start | bytes 11796480 | tf_op jit(solution)/shard_map/reduce_scatter | solution.py:237
  982.6 28.7 %copy-start.156 = (bf16[2,768,768]{2,1,0:T(8,128)(2,1)S(1)}, bf16[2,768,768]{2,1,0:T(8,128)(2,1)}, u32[]{:S(2)}) copy-start(bf16[2,768,768]{2,1,0:T(8,128)(2,1)} %param.44) | copy-start | bytes 7077892
  1100.4 34.1 %all-to-all-start.3 = ((bf16[1,2,384,768]{3,1,0,2:T(2,128)(2,1)}), bf16[1,2,384,768]{3,1,0,2:T(2,128)(2,1)S(1)}, u32[]{:S(2)}, u32[]{:S(2)}) async-start(bf16[1,2,384,768]{3,1,0,2:T(2,128)(2,1)} %copy.114), calls=%async_computation.5 | async-start | bytes 2359296 | tf_op jit(solution)/shard_map/all_to_all | solution.py:238
  1105.9 749.8 %all-reduce.76.cloned.1.call-start = ((), (), s32[]{:S(2)}) async-start(), calls=%async_computation.12 | async-start | bytes 215040 | tf_op jit(solution)/shard_map/psum | solution.py:261
  1469.0 15.4 copy-start.79
  1469.0 17.6 copy-start.26
  1469.1 17.6 slice-start.8
  1827.1 297.4 %all-reduce.78.cloned.1.call-start = ((), (), s32[]{:S(2)}) async-start(), calls=%async_computation.13 | async-start | bytes 30081024 | tf_op jit(solution)/shard_map/psum | solution.py:261
  1830.8 369.0 %all-reduce.72.cloned.1.call-start = ((), (), s32[]{:S(2)}) async-start(), calls=%async_computation.10 | async-start | bytes 215040 | tf_op jit(solution)/shard_map/psum | solution.py:260
  1855.8 816.0 %all-reduce.74.cloned.1.call-start = ((), (), s32[]{:S(2)}) async-start(), calls=%async_computation.11 | async-start | bytes 30081024 | tf_op jit(solution)/shard_map/psum | solution.py:260
  2134.6 25.3 copy-start.127
  2134.6 25.3 copy-start.28
  2134.6 25.3 copy-start.48
  2134.6 25.3 copy-start.76
  2671.8 14.8 slice-start.5
  (280 other events, 1081.5 us)
Sparse Core Ops, SparseCore 0:
  719.6 36.1 all-gather.3
  792.1 78.4 reduce-scatter.2
  947.4 35.2 all-gather.5
  1017.8 78.4 reduce-scatter.4
  1827.2 28.4 all-reduce.75
  1860.6 263.8 all-reduce.77
  2128.9 70.8 all-reduce.71
  2205.9 465.8 all-reduce.73
